TPU v7x, 32 devices: a whole 2x2x4 slice. The times are simulated.
32 devices in a mesh: design: 8 (over z, x), feat: 4 (over y, core).
Axes of the slice: x: 2, y: 2, z: 4, core: 2. Of those that a mesh axis runs over, the one named last changes fastest.
Arguments:
- table: bfloat16 [32768, 1024], P('design', 'feat'), may hold values from -0.29882812 to 0.29882812
- proj_weight: float32 [1024, 128], P('feat'), may hold values from -0.1875 to 0.1875
- anchor_ids: int32 [4096], P('design'), may hold values from 0 to 32767, as said below
- positive_ids: int32 [4096], P('design'), may hold values from 0 to 32767, as said below
- neg_tiles: int32 [32, 16], P('design'), may hold values from 0 to 255, as said below
Outputs:
- losses: float32 [4096], P('design')
- table_grad: float32 [32768, 1024], P('design', 'feat')
- weight_grad: float32 [1024, 128], P('feat')
Inputs may be any that keep to these rules, and one draw needn't show every extreme that they name: `anchor_ids`: entry i lies in the rows held by design index i // 512, that is from that index times 4096 on, 4096 rows. `positive_ids`: entry i lies in the rows held by design index i // 512, that is from that index times 4096 on, 4096 rows. `neg_tiles`: tile t is held by design index t // 32. Among the 4 rows of blocks of one design index, at most 16 entries name tiles held by any one index, and exactly 16 for some index.
All inputs are finite; a program needn't handle non-finite values.
Results may differ from a plain program's by a relative error of at most 0.0004.
Values may be sent and summed in bfloat16 or wider, within the bound.
A program may use at most 192 MiB of HBM per device.

v0:
```python
import jax
import jax.numpy as jnp
from jax import lax
from jax.sharding import PartitionSpec as P

TILE = 128
SOFTMAX_TEMP = 0.07
EPSILON = 1e-06


def unit_rows(values):
    return values / jnp.sqrt(jnp.sum(values * values, axis=-1, keepdims=True) + EPSILON)


def block_losses(anchor_z, positive_z, negative_z):
    anchor_unit_vector = unit_rows(anchor_z)
    positive_unit_vector = unit_rows(positive_z)
    negative_unit_vector = unit_rows(negative_z)
    positive_similarity = jnp.sum(anchor_unit_vector * positive_unit_vector, axis=-1) / SOFTMAX_TEMP
    negative_similarity = (
        jnp.einsum(
            "kjc,koc->kjo",
            anchor_unit_vector,
            negative_unit_vector,
            precision=lax.Precision.HIGHEST,
        )
        / SOFTMAX_TEMP
    )
    total = jnp.exp(positive_similarity) + jnp.sum(jnp.exp(negative_similarity), axis=-1)
    return jnp.log(total) - positive_similarity


def full_dot(left, right):
    return jnp.dot(left, right, precision=lax.Precision.HIGHEST, preferred_element_type=jnp.float32)


def shards(table, proj_weight, anchor_ids, positive_ids, neg_tiles):
    n_design = lax.axis_size("design")
    my_index = lax.axis_index("design")
    shard_rows, width = table.shape
    code_width = proj_weight.shape[1]
    tiles_dev = shard_rows // TILE
    blocks, negs = neg_tiles.shape
    wanted = blocks * negs
    capacity = 2 * wanted // n_design
    slot_count = n_design * capacity
    anchor_local = anchor_ids - my_index * shard_rows
    positive_local = positive_ids - my_index * shard_rows
    flat_tiles = neg_tiles.reshape(wanted)
    owner_dev = flat_tiles // tiles_dev
    local_tile = flat_tiles - owner_dev * tiles_dev
    request_order = jnp.arange(wanted, dtype=jnp.int32)
    earlier = (owner_dev[:, None] == owner_dev[None, :]) & (
        request_order[:, None] < request_order[None, :]
    )
    slot_rank = jnp.sum(earlier.astype(jnp.int32), axis=0)
    slot_position = owner_dev * capacity + slot_rank
    request = jnp.zeros((slot_count,), jnp.int32).at[slot_position].set(local_tile)
    asked = lax.all_to_all(
        request.reshape(n_design, capacity), "design", split_axis=0, concat_axis=0, tiled=True
    ).reshape(slot_count)
    own_embed = table.astype(jnp.float32)
    anchor_part = full_dot(own_embed[anchor_local], proj_weight)
    positive_part = full_dot(own_embed[positive_local], proj_weight)
    anchor_z, positive_z = lax.psum((anchor_part, positive_part), "feat")
    outgoing = table.reshape(tiles_dev, TILE, width)[asked].reshape(n_design, capacity, TILE, width)
    arrived = lax.all_to_all(outgoing, "design", split_axis=0, concat_axis=0, tiled=True).reshape(
        slot_count, TILE, width
    )
    negative_embed = arrived[slot_position].reshape(wanted * TILE, width).astype(jnp.float32)
    negative_z = lax.psum(full_dot(negative_embed, proj_weight), "feat")
    losses, pullback = jax.vjp(
        block_losses,
        anchor_z.reshape(blocks, TILE, code_width),
        positive_z.reshape(blocks, TILE, code_width),
        negative_z.reshape(blocks, negs * TILE, code_width),
    )
    anchor_grad, positive_grad, negative_grad = pullback(jnp.ones_like(losses))
    code_grad = jnp.zeros((shard_rows, code_width), jnp.float32)
    code_grad = code_grad.at[anchor_local].add(anchor_grad.reshape(-1, code_width))
    code_grad = code_grad.at[positive_local].add(positive_grad.reshape(-1, code_width))
    negative_tiles_grad = negative_grad.reshape(wanted, TILE, code_width)
    negative_rows_grad = negative_tiles_grad.reshape(wanted * TILE, code_width)
    embed_grad = full_dot(negative_rows_grad, proj_weight.T).reshape(wanted, TILE, width)
    weight_part = full_dot(own_embed.T, code_grad) + full_dot(negative_embed.T, negative_rows_grad)
    send_back = jnp.zeros((slot_count, TILE, width), jnp.float32).at[slot_position].set(embed_grad)
    returned = lax.all_to_all(
        send_back.reshape(n_design, capacity, TILE, width).astype(jnp.bfloat16),
        "design",
        split_axis=0,
        concat_axis=0,
        tiled=True,
    ).astype(jnp.float32)
    table_grad = full_dot(code_grad, proj_weight.T).reshape(tiles_dev, TILE, width)
    table_grad = (
        table_grad.at[asked]
        .add(returned.reshape(slot_count, TILE, width))
        .reshape(shard_rows, width)
    )
    weight_grad = lax.psum(weight_part, "design")
    return (losses.reshape(blocks * TILE), table_grad, weight_grad)


def solution(mesh):
    in_specs = (P("design", "feat"), P("feat", None), P("design"), P("design"), P("design", None))
    out_specs = (P("design"), P("design", "feat"), P("feat", None))
    return jax.shard_map(shards, mesh=mesh, in_specs=in_specs, out_specs=out_specs, check_vma=False)
```

profile of v0, /device:TPU:8, one launch (start us, length us, event | category | flops | bytes accessed | tf_op | source)
XLA Modules:
  0.0 666.7 jit_solution(4649962688690059816)
XLA Ops:
  7.2 0.0 copy-start
  7.2 0.9 reshape.332
  8.1 0.8 reshape.331
  8.9 0.1 convert_reduce_fusion
  9.0 0.8 scatter_custom_fusion
  9.8 0.1 all_to_all.12
  9.8 11.1 %all_to_all.19 = s32[8,1,16]{2,1,0:T(1,128)S(1)} all-to-all(s32[8,1,16]{2,1,0:T(1,128)S(1)} %bitcast.88), channel_id=1, replica_groups=mesh['design'=8,'feat'=4] {'design'}, dimensions={0} | all-to-all | bytes 1024 | tf_op jit(solution)/shard_map/all_to_all | solution.py:59
  20.9 0.5 broadcast.326
  21.4 0.7 reduce.8
  22.1 0.1 reshape.333
  22.2 0.0 copy-done
  22.2 6.2 gather_fusion.2
  28.4 0.0 copy-start.8
  28.4 6.6 all-to-all-start.1
  35.1 0.0 all-reduce.6.cloned.1.call-start
  35.1 0.0 copy-done.8
  35.1 0.0 copy-done.9
  35.1 2.0 gather_fusion
  37.1 2.0 gather_fusion.1
  39.1 0.0 copy-done.7
  39.1 1.1 fusion.32
  40.1 1.1 fusion.33
  41.2 173.3 %all-to-all-done.1 = bf16[8,16,128,256]{3,2,1,0:T(8,128)(2,1)} async-done(((bf16[8,16,128,256]{3,2,1,0:T(8,128)(2,1)}), bf16[8,16,128,256]{3,2,1,0:T(8,128)(2,1)}, u32[]{:S(2)}, u32[]{:S(2)}) %all-to-all-start.1) | async-done | bytes 8388640 | tf_op jit(solution)/shard_map/all_to_all | solution.py:67
  214.5 6.2 gather_fusion.3
  220.7 7.5 %fusion.34 = f32[8192,128]{1,0:T(8,128)} fusion(bf16[8192,256]{1,0:T(8,128)(2,1)} %bitcast.74, f32[256,128]{1,0:T(8,128)S(1)} %copy-done.7), kind=kOutput, calls=%fused_computation.98 | convolution fusion | flops 3221225472 | bytes 8519680 | tf_op jit(solution)/shard_map/dot_general | solution.py:34
  228.3 0.0 all-reduce.6.cloned.1.call-update
  228.3 95.3 %all-reduce.6.cloned.1.call-done = (f32[8192,128]{1,0:T(8,128)}, f32[512,128]{1,0:T(8,128)}, f32[512,128]{1,0:T(8,128)}) async-done(((f32[8192,128]{1,0:T(8,128)}, f32[512,128]{1,0:T(8,128)}, f32[512,128]{1,0:T(8,128)}), (f32[8192,128]{1,0:T(8,128)}, f32[512,128]{1,0:T(8,128)}, f32[512,128]{1,0:T(8,128)})) %all-reduce.6.cloned.1.call-update) | async-done | bytes 4718608 | tf_op jit(solution)/shard_map/psum | solution.py:71
  323.6 1.2 multiply_reduce_fusion.6
  324.8 1.1 multiply_reduce_fusion.5
  325.9 3.3 multiply_reduce_fusion.1
  329.3 0.0 copy-done.4
  329.3 0.0 copy-done.5
  329.3 0.3 multiply_reduce_fusion.4
  329.7 7.1 %fusion = (f32[4,128]{1,0:T(4,128)S(1)}, f32[4,128,2048]{2,1,0:T(8,128)S(1)}) fusion(f32[4,2048,128]{2,1,0:T(8,128)} %bitcast.78, f32[4,2048]{1,0:T(4,128)S(1)} %sqrt.60, f32[4,128,128]{2,1,0:T(8,128)S(1)} %bitcast.83, f32[4,128]{1,0:T(4,128)S(1)} %get-tuple-element.28), kind=kOutput, calls=%fused_computation.15 | convolution fusion | flops 1613823488 | bytes 8687616 | tf_op jit(solution)/shard_map/jvp(kjc,koc->kjo)/dot_general | solution.py:21
  336.8 0.0 copy-start.6
  336.8 0.0 copy-done.3
  336.8 9.8 %multiply_reduce_fusion = (f32[4,2048]{1,0:T(4,128)S(1)}, f32[4,2048,128]{2,1,0:T(8,128)S(1)}) fusion(f32[4,2048,128]{2,1,0:T(8,128)S(1)} %bitcast.80, f32[4,2048]{1,0:T(4,128)S(1)} %multiply_divide_fusion, f32[4,128,128]{2,1,0:T(8,128)S(1)} %bitcast.84, f32[4,128]{1,0:T(4,128)S(1)} %get-tuple-element.28, f32[4,128,2048]{2,1,0:T(8,128)S(1)} %get-tuple-element.30, ...), kind=kOutput, calls=%fused_computation.11 | convolution fusion | flops 1616961536 | bytes 12914688 | tf_op jit(solution)/shard_map/transpose(jvp(kjc,koc->kjo))/dot_general | solution.py:21
  346.7 0.0 copy-done.6
  346.7 2.5 add_add_fusion
  349.2 0.0 copy-start.2
  349.2 1.9 copy-done.2
  351.1 8.9 %fusion.15 = f32[64,128,256]{2,1,0:T(8,128)} fusion(f32[64,128,128]{2,1,0:T(8,128)S(1)} %bitcast.76, f32[256,128]{1,0:T(8,128)S(1)} %copy-done.7), kind=kOutput, calls=%fused_computation.40 | convolution fusion | flops 3221225472 | bytes 12713984 | tf_op jit(solution)/shard_map/dot_general | solution.py:34
  360.0 7.8 %broadcast_in_dim.61 = f32[128,128,256]{2,1,0:T(8,128)} broadcast(f32[]{:T(128)} %constant.21.clone.1), dimensions={} | broadcast | bytes 16777220 | tf_op jit(solution)/shard_map/broadcast_in_dim | solution.py:86
  367.9 16.1 %scatter_fusion = f32[128,128,256]{2,1,0:T(8,128)} fusion(f32[128,128,256]{2,1,0:T(8,128)} %broadcast_in_dim.61, s32[64]{0:T(128)S(1)} %fusion.24, f32[64,128,256]{2,1,0:T(8,128)} %fusion.15), kind=kCustom, calls=%fused_computation.7 | custom fusion | bytes 25166080 | tf_op jit(solution)/shard_map/scatter | solution.py:86
  384.0 9.0 %convert_element_type.13 = bf16[128,128,256]{2,1,0:T(8,128)(2,1)} convert(f32[128,128,256]{2,1,0:T(8,128)} %scatter_fusion) | non-fusion elementwise | flops 4194304 | bytes 25165824 | tf_op jit(solution)/shard_map/convert_element_type | solution.py:88
  392.9 6.2 all-to-all-start.2
  399.2 0.0 all-reduce.4.cloned.1.call-start
  399.2 0.6 add_multiply_fusion
  399.8 0.4 multiply_reduce_fusion.2
  400.2 8.0 %multiply_reduce_fusion.3 = (f32[4,128]{1,0:T(4,128)S(1)}, f32[4,128,128]{2,1,0:T(8,128)S(1)}) fusion(f32[4,128,128]{2,1,0:T(8,128)S(1)} %bitcast.85, f32[4,128]{1,0:T(4,128)S(1)} %multiply_divide_fusion.2, f32[4,128,128]{2,1,0:T(8,128)S(1)} %bitcast.86, f32[4,128]{1,0:T(4,128)S(1)} %get-tuple-element.24, f32[4,128]{1,0:T(4,128)S(1)} %get-tuple-element.21, ...), kind=kOutput, calls=%fused_computation.35 | convolution fusion | flops 1615199744 | bytes 9218048 | tf_op jit(solution)/shard_map/transpose(jvp(kjc,koc->kjo))/dot_general | solution.py:21
  408.2 0.2 add_add_fusion.2
  408.4 3.6 scatter_custom_fusion.1
  412.1 6.4 scatter_custom_fusion.2
  418.5 0.0 copy-start.1
  418.5 3.5 convolution_bitcast_fusion
  422.0 0.0 copy-done.1
  422.0 6.4 convolution_add_fusion
  428.5 0.0 all-reduce.4.cloned.1.call-update
  428.5 7.0 %fusion.35 = f32[4096,256]{1,0:T(8,128)} fusion(f32[4096,128]{1,0:T(8,128)} %scatter_custom_fusion.2, f32[256,128]{1,0:T(8,128)S(1)} %copy-done.7), kind=kOutput, calls=%fused_computation.99 | convolution fusion | flops 1610612736 | bytes 6422528 | tf_op jit(solution)/shard_map/dot_general | solution.py:34
  435.6 168.4 %all-reduce.4.cloned.1.call-done = f32[256,128]{0,1:T(8,128)} async-done(((f32[256,128]{0,1:T(8,128)}), f32[256,128]{0,1:T(8,128)}) %all-reduce.4.cloned.1.call-update) | async-done | bytes 131088 | tf_op jit(solution)/shard_map/psum | solution.py:100
  603.9 1.7 copy.18
  605.6 0.0 all-to-all-done.2
  605.6 11.5 %bitcast_convert_fusion = f32[128,128,256]{2,1,0:T(8,128)} fusion(bf16[8,16,128,256]{3,2,1,0:T(8,128)(2,1)} %all-to-all-done.2), kind=kLoop, calls=%fused_computation.9 | loop fusion | flops 4194304 | bytes 25165824 | tf_op jit(solution)/shard_map/reshape | solution.py:97
  617.0 42.6 %scatter_fusion.1 = f32[32,128,256]{2,1,0:T(8,128)} fusion(f32[32,128,256]{2,1,0:T(8,128)} %bitcast.72, s32[128]{0:T(128)S(1)} %fusion.25, f32[128,128,256]{2,1,0:T(8,128)} %bitcast_convert_fusion), kind=kCustom, calls=%fused_computation.8 | custom fusion | flops 4194304 | bytes 50332160 | tf_op jit(solution)/shard_map/scatter-add | solution.py:97
  (24 shorter events, 0.2 us)
Async XLA Ops:
  7.2 15.0 %copy-start = (bf16[4096,256]{1,0:T(8,128)(2,1)S(1)}, bf16[4096,256]{1,0:T(8,128)(2,1)}, u32[]{:S(2)}) copy-start(bf16[4096,256]{1,0:T(8,128)(2,1)} %param.5) | copy-start | bytes 6291460
  28.4 6.7 copy-start.8
  28.4 6.7 copy-start.9
  28.4 186.1 %all-to-all-start.1 = ((bf16[8,16,128,256]{3,2,1,0:T(8,128)(2,1)}), bf16[8,16,128,256]{3,2,1,0:T(8,128)(2,1)}, u32[]{:S(2)}, u32[]{:S(2)}) async-start(bf16[8,16,128,256]{3,2,1,0:T(8,128)(2,1)} %bitcast.82), calls=%async_computation.1 | async-start | bytes 16777216 | tf_op jit(solution)/shard_map/all_to_all | solution.py:67
  35.1 4.0 copy-start.7
  35.1 288.5 %all-reduce.6.cloned.1.call-start = ((), (), s32[]{:S(2)}) async-start(), calls=%async_computation.4 | async-start | bytes 9437184 | tf_op jit(solution)/shard_map/psum | solution.py:71
  323.6 5.7 copy-start.4
  323.6 5.8 copy-start.5
  329.6 7.2 %copy-start.3 = (f32[8192,128]{1,0:T(8,128)S(1)}, f32[8192,128]{1,0:T(8,128)}, u32[]{:S(2)}) copy-start(f32[8192,128]{1,0:T(8,128)} %get-tuple-element.12) | copy-start | bytes 12582916
  336.8 9.9 %copy-start.6 = (f32[4,128,2048]{2,1,0:T(8,128)}, f32[4,128,2048]{2,1,0:T(8,128)S(1)}, u32[]{:S(2)}) copy-start(f32[4,128,2048]{2,1,0:T(8,128)S(1)} %get-tuple-element.30) | copy-start | bytes 12582916
  349.2 1.9 copy-start.2
  392.9 212.6 %all-to-all-start.2 = ((bf16[8,16,128,256]{3,2,1,0:T(8,128)(2,1)}), bf16[8,16,128,256]{3,2,1,0:T(8,128)(2,1)}, u32[]{:S(2)}, u32[]{:S(2)}) async-start(bf16[8,16,128,256]{3,2,1,0:T(8,128)(2,1)} %bitcast.81), calls=%async_computation.2 | async-start | bytes 16777216 | tf_op jit(solution)/shard_map/all_to_all | solution.py:87
  399.2 204.7 %all-reduce.4.cloned.1.call-start = ((), (), s32[]{:S(2)}) async-start(), calls=%async_computation.3 | async-start | bytes 262144 | tf_op jit(solution)/shard_map/psum | solution.py:100
  418.5 3.6 copy-start.1
Sparse Core Ops, SparseCore 0:
  228.4 95.0 all-reduce.5
  428.6 175.2 all-reduce.3
where the time goes:
time: 676 us; the launch traced here: 667 us
  waiting for transfers between devices  437 us (65%)
  other arithmetic  83.6 us (12%)
  matrix products  60.6 us (9%)
  local copies, waits for them, and re-layouts  47 us (7%)
  between operations  14.6 us (2%)
  starting transfers between devices  12.9 us (2%)
  blocking collectives  11.1 us (2%)
    all_to_all x1, waiting for transfers between devices, shards(): lax.all_to_all(outgoing, 'design', split_axis=0, concat_axis=0, tiled=True)  173 us
    psum x1, waiting for transfers between devices, shards(): weight_grad = lax.psum(weight_part, 'design')  168 us
    psum x1, waiting for transfers between devices, shards(): negative_z = lax.psum(full_dot(negative_embed, proj_weight), 'feat')  95.3 us
    scatter-add x1, other arithmetic, shards(): table_grad = table_grad.at[asked].add(returned.reshape(slot_count, TILE,...  42.6 us
    dot_general x7, matrix products, full_dot(): jnp.dot(left, right, precision=lax.Precision.HIGHEST, preferred_element_t...  35.6 us
    dot_general x3, matrix products, block_losses(): jnp.einsum('kjc,koc->kjo', anchor_unit_vector, negative_unit_vector, prec...  25 us
    scatter x1, local copies, waits for them, and re-layouts, shards(): jnp.zeros((slot_count, TILE, width), jnp.float32).at[slot_position]  16.1 us
  transfers between devices with their start and end apart: 4, of which 3 were waited for; matrix products, arithmetic and copies ran while one was open for 7% of the time, Pallas kernels for 0%

commit v1 on v0

--- a/solution.py
+++ b/solution.py
@@ -97,7 +97,11 @@
         .add(returned.reshape(slot_count, TILE, width))
         .reshape(shard_rows, width)
     )
-    weight_grad = lax.psum(weight_part, "design")
+    weight_grad = weight_part
+    for hop in (1, 2, 4):
+        weight_grad = weight_grad + lax.ppermute(
+            weight_grad, "design", [(dev, dev ^ hop) for dev in range(8)]
+        )
     return (losses.reshape(blocks * TILE), table_grad, weight_grad)
 
 

time: 676 us -> 655 us (0.969)
  waiting for transfers between devices: 437 us -> 417 us
    psum x1 -> x0, waiting for transfers between devices: 168 us -> none  [shards(): weight_grad = lax.psum(weight_part, 'design')]
    ppermute x0 -> x3, waiting for transfers between devices: none -> 148 us  [shards(): lax.ppermute(weight_grad, 'design', [(dev, dev ^ hop) for dev in range(8)])]
  transfers between devices with their start and end apart: 4 -> 6, of which waited for: 3 -> 5; matrix products, arithmetic and copies ran while one was open for 7% -> 6% of each run, Pallas kernels for 0% -> 0%
where the time goes in v1:
time: 655 us; the launch traced here: 646 us
  waiting for transfers between devices  417 us (64%)
  other arithmetic  82.7 us (13%)
  matrix products  57.8 us (9%)
  local copies, waits for them, and re-layouts  46.1 us (7%)
  starting transfers between devices  16.9 us (3%)
  between operations  14.6 us (2%)
  blocking collectives  11.1 us (2%)
    all_to_all x1, waiting for transfers between devices, shards(): lax.all_to_all(outgoing, 'design', split_axis=0, concat_axis=0, tiled=True)  173 us
    ppermute x3, waiting for transfers between devices, shards(): lax.ppermute(weight_grad, 'design', [(dev, dev ^ hop) for dev in range(8)])  148 us
    psum x1, waiting for transfers between devices, shards(): negative_z = lax.psum(full_dot(negative_embed, proj_weight), 'feat')  95.3 us
    scatter-add x1, other arithmetic, shards(): table_grad = table_grad.at[asked].add(returned.reshape(slot_count, TILE,...  42.6 us
    dot_general x7, matrix products, full_dot(): jnp.dot(left, right, precision=lax.Precision.HIGHEST, preferred_element_t...  33 us
    dot_general x3, matrix products, block_losses(): jnp.einsum('kjc,koc->kjo', anchor_unit_vector, negative_unit_vector, prec...  24.8 us
    scatter x1, local copies, waits for them, and re-layouts, shards(): jnp.zeros((slot_count, TILE, width), jnp.float32).at[slot_position]  16.1 us
  transfers between devices with their start and end apart: 6, of which 5 were waited for; matrix products, arithmetic and copies ran while one was open for 6% of the time, Pallas kernels for 0%

profile of v1, /device:TPU:8, one launch (start us, length us, event | category | flops | bytes accessed | tf_op | source)
XLA Modules:
  0.0 646.1 jit_solution(11937054193899511719)
XLA Ops:
  7.2 0.0 copy-start
  7.2 0.9 reshape.332
  8.1 0.8 reshape.331
  8.9 0.1 convert_reduce_fusion
  9.0 0.8 scatter_custom_fusion
  9.8 0.1 all_to_all.12
  9.8 11.1 %all_to_all.19 = s32[8,1,16]{2,1,0:T(1,128)S(1)} all-to-all(s32[8,1,16]{2,1,0:T(1,128)S(1)} %bitcast.86), channel_id=1, replica_groups=mesh['design'=8,'feat'=4] {'design'}, dimensions={0} | all-to-all | bytes 1024 | tf_op jit(solution)/shard_map/all_to_all | solution.py:59
  20.9 0.5 broadcast.326
  21.4 0.7 reduce.8
  22.1 0.1 reshape.333
  22.2 0.0 copy-done
  22.2 6.2 gather_fusion.2
  28.4 6.6 %all-to-all-start.1 = ((bf16[8,16,128,256]{3,2,1,0:T(8,128)(2,1)}), bf16[8,16,128,256]{3,2,1,0:T(8,128)(2,1)}, u32[]{:S(2)}, u32[]{:S(2)}) async-start(bf16[8,16,128,256]{3,2,1,0:T(8,128)(2,1)} %bitcast.80), calls=%async_computation.1 | async-start | bytes 16777216 | tf_op jit(solution)/shard_map/all_to_all | solution.py:67
  35.1 0.0 all-reduce.3.cloned.1.call-start
  35.1 0.0 copy-done.9
  35.1 0.0 copy-done.10
  35.1 2.0 gather_fusion
  37.1 2.0 gather_fusion.1
  39.1 0.0 copy-done.8
  39.1 1.1 fusion.32
  40.1 1.1 fusion.33
  41.2 173.3 %all-to-all-done.1 = bf16[8,16,128,256]{3,2,1,0:T(8,128)(2,1)} async-done(((bf16[8,16,128,256]{3,2,1,0:T(8,128)(2,1)}), bf16[8,16,128,256]{3,2,1,0:T(8,128)(2,1)}, u32[]{:S(2)}, u32[]{:S(2)}) %all-to-all-start.1) | async-done | bytes 8388640 | tf_op jit(solution)/shard_map/all_to_all | solution.py:67
  214.5 6.2 gather_fusion.3
  220.7 7.5 %fusion.34 = f32[8192,128]{1,0:T(8,128)} fusion(bf16[8192,256]{1,0:T(8,128)(2,1)} %bitcast.72, f32[256,128]{1,0:T(8,128)S(1)} %copy-done.8), kind=kOutput, calls=%fused_computation.98 | convolution fusion | flops 3221225472 | bytes 8519680 | tf_op jit(solution)/shard_map/dot_general | solution.py:34
  228.3 0.0 all-reduce.3.cloned.1.call-update
  228.3 95.3 %all-reduce.3.cloned.1.call-done = (f32[8192,128]{1,0:T(8,128)}, f32[512,128]{1,0:T(8,128)}, f32[512,128]{1,0:T(8,128)}) async-done(((f32[8192,128]{1,0:T(8,128)}, f32[512,128]{1,0:T(8,128)}, f32[512,128]{1,0:T(8,128)}), (f32[8192,128]{1,0:T(8,128)}, f32[512,128]{1,0:T(8,128)}, f32[512,128]{1,0:T(8,128)})) %all-reduce.3.cloned.1.call-update) | async-done | bytes 4718608 | tf_op jit(solution)/shard_map/psum | solution.py:71
  323.6 1.2 multiply_reduce_fusion.6
  324.8 3.3 multiply_reduce_fusion.1
  328.2 0.1 multiply_reduce_fusion.5
  328.4 0.3 multiply_reduce_fusion.4
  328.7 7.2 %fusion = (f32[4,128]{1,0:T(4,128)S(1)}, f32[4,128,2048]{2,1,0:T(8,128)S(1)}) fusion(f32[4,2048,128]{2,1,0:T(8,128)} %bitcast.76, f32[4,2048]{1,0:T(4,128)S(1)} %sqrt.60, f32[4,128,128]{2,1,0:T(8,128)S(1)} %bitcast.81, f32[4,128]{1,0:T(4,128)S(1)} %get-tuple-element.28), kind=kOutput, calls=%fused_computation.15 | convolution fusion | flops 1613823488 | bytes 8687616 | tf_op jit(solution)/shard_map/jvp(kjc,koc->kjo)/dot_general | solution.py:21
  335.9 0.0 copy-done.3
  335.9 9.8 %multiply_reduce_fusion = (f32[4,2048]{1,0:T(4,128)S(1)}, f32[4,2048,128]{2,1,0:T(8,128)S(1)}) fusion(f32[4,2048,128]{2,1,0:T(8,128)S(1)} %bitcast.78, f32[4,2048]{1,0:T(4,128)S(1)} %multiply_divide_fusion, f32[4,128,128]{2,1,0:T(8,128)S(1)} %bitcast.82, f32[4,128]{1,0:T(4,128)S(1)} %get-tuple-element.28, f32[4,128,2048]{2,1,0:T(8,128)S(1)} %get-tuple-element.30, ...), kind=kOutput, calls=%fused_computation.11 | convolution fusion | flops 1616961536 | bytes 12914688 | tf_op jit(solution)/shard_map/transpose(jvp(kjc,koc->kjo))/dot_general | solution.py:21
  345.7 2.5 add_add_fusion
  348.3 0.0 copy-start.2
  348.3 1.9 copy-done.2
  350.2 8.9 %fusion.15 = f32[64,128,256]{2,1,0:T(8,128)} fusion(f32[64,128,128]{2,1,0:T(8,128)S(1)} %bitcast.74, f32[256,128]{1,0:T(8,128)S(1)} %copy-done.8), kind=kOutput, calls=%fused_computation.40 | convolution fusion | flops 3221225472 | bytes 12713984 | tf_op jit(solution)/shard_map/dot_general | solution.py:34
  359.1 7.8 %broadcast_in_dim.61 = f32[128,128,256]{2,1,0:T(8,128)} broadcast(f32[]{:T(128)} %constant.21.clone.1), dimensions={} | broadcast | bytes 16777220 | tf_op jit(solution)/shard_map/broadcast_in_dim | solution.py:86
  366.9 16.1 %scatter_fusion = f32[128,128,256]{2,1,0:T(8,128)} fusion(f32[128,128,256]{2,1,0:T(8,128)} %broadcast_in_dim.61, s32[64]{0:T(128)S(1)} %fusion.24, f32[64,128,256]{2,1,0:T(8,128)} %fusion.15), kind=kCustom, calls=%fused_computation.7 | custom fusion | bytes 25166080 | tf_op jit(solution)/shard_map/scatter | solution.py:86
  383.0 9.0 %convert_element_type.13 = bf16[128,128,256]{2,1,0:T(8,128)(2,1)} convert(f32[128,128,256]{2,1,0:T(8,128)} %scatter_fusion) | non-fusion elementwise | flops 4194304 | bytes 25165824 | tf_op jit(solution)/shard_map/convert_element_type | solution.py:88
  392.0 6.4 all-to-all-start.2
  398.4 0.6 add_multiply_fusion
  399.0 0.4 multiply_reduce_fusion.2
  399.4 7.8 %multiply_reduce_fusion.3 = (f32[4,128]{1,0:T(4,128)S(1)}, f32[4,128,128]{2,1,0:T(8,128)S(1)}) fusion(f32[4,128,128]{2,1,0:T(8,128)S(1)} %bitcast.83, f32[4,128]{1,0:T(4,128)S(1)} %multiply_divide_fusion.2, f32[4,128,128]{2,1,0:T(8,128)S(1)} %bitcast.84, f32[4,128]{1,0:T(4,128)S(1)} %get-tuple-element.24, f32[4,128]{1,0:T(4,128)S(1)} %get-tuple-element.21, ...), kind=kOutput, calls=%fused_computation.35 | convolution fusion | flops 1615199744 | bytes 9218048 | tf_op jit(solution)/shard_map/transpose(jvp(kjc,koc->kjo))/dot_general | solution.py:21
  407.3 0.2 add_add_fusion.2
  407.5 3.6 scatter_custom_fusion.1
  411.1 6.4 scatter_custom_fusion.2
  417.6 0.0 copy-start.1
  417.6 3.5 convolution_bitcast_fusion
  421.1 0.0 copy-done.1
  421.1 0.0 copy-start.4
  421.1 5.9 convolution_add_fusion
  427.1 1.5 collective-permute-start
  428.6 39.5 %collective-permute-done = f32[256,128]{0,1:T(8,128)S(1)} collective-permute-done((f32[256,128]{0,1:T(8,128)S(1)}, f32[256,128]{0,1:T(8,128)S(1)}, u32[]{:S(2)}, u32[]{:S(2)}) %collective-permute-start) | collective-permute-done | bytes 131104 | tf_op jit(solution)/shard_map/ppermute | solution.py:102
  468.2 1.5 collective-permute-start.1
  469.6 67.6 %collective-permute-done.1 = f32[256,128]{0,1:T(8,128)S(1)} collective-permute-done((f32[256,128]{0,1:T(8,128)S(1)}, f32[256,128]{0,1:T(8,128)S(1)}, u32[]{:S(2)}, u32[]{:S(2)}) %collective-permute-start.1) | collective-permute-done | bytes 131104 | tf_op jit(solution)/shard_map/ppermute | solution.py:102
  537.2 0.9 collective-permute-start.2
  538.1 0.0 copy-done.4
  538.1 4.9 fusion.35
  543.0 41.1 %collective-permute-done.2 = f32[256,128]{0,1:T(8,128)S(1)} collective-permute-done((f32[256,128]{0,1:T(8,128)S(1)}, f32[256,128]{0,1:T(8,128)S(1)}, u32[]{:S(2)}, u32[]{:S(2)}) %collective-permute-start.2) | collective-permute-done | bytes 131104 | tf_op jit(solution)/shard_map/ppermute | solution.py:102
  584.1 0.8 copy.18
  584.9 0.0 all-to-all-done.2
  584.9 11.5 %bitcast_convert_fusion = f32[128,128,256]{2,1,0:T(8,128)} fusion(bf16[8,16,128,256]{3,2,1,0:T(8,128)(2,1)} %all-to-all-done.2), kind=kLoop, calls=%fused_computation.9 | loop fusion | flops 4194304 | bytes 25165824 | tf_op jit(solution)/shard_map/reshape | solution.py:97
  596.4 42.6 %scatter_fusion.1 = f32[32,128,256]{2,1,0:T(8,128)} fusion(f32[32,128,256]{2,1,0:T(8,128)} %bitcast.70, s32[128]{0:T(128)S(1)} %fusion.25, f32[128,128,256]{2,1,0:T(8,128)} %bitcast_convert_fusion), kind=kCustom, calls=%fused_computation.8 | custom fusion | flops 4194304 | bytes 50332160 | tf_op jit(solution)/shard_map/scatter-add | solution.py:97
  (32 shorter events, 0.3 us)
Async XLA Ops:
  7.2 15.0 %copy-start = (bf16[4096,256]{1,0:T(8,128)(2,1)S(1)}, bf16[4096,256]{1,0:T(8,128)(2,1)}, u32[]{:S(2)}) copy-start(bf16[4096,256]{1,0:T(8,128)(2,1)} %param.5) | copy-start | bytes 6291460
  28.4 6.7 %copy-start.9 = (s32[512]{0:T(512)S(1)}, s32[512]{0:T(512)}, u32[]{:S(2)}) copy-start(s32[512]{0:T(512)} %param.8) | copy-start | bytes 6148
  28.4 6.7 %copy-start.10 = (s32[512]{0:T(512)S(1)}, s32[512]{0:T(512)}, u32[]{:S(2)}) copy-start(s32[512]{0:T(512)} %param.7) | copy-start | bytes 6148
  28.4 186.1 %all-to-all-start.1 = ((bf16[8,16,128,256]{3,2,1,0:T(8,128)(2,1)}), bf16[8,16,128,256]{3,2,1,0:T(8,128)(2,1)}, u32[]{:S(2)}, u32[]{:S(2)}) async-start(bf16[8,16,128,256]{3,2,1,0:T(8,128)(2,1)} %bitcast.80), calls=%async_computation.1 | async-start | bytes 16777216 | tf_op jit(solution)/shard_map/all_to_all | solution.py:67
  35.1 4.0 copy-start.8
  35.1 288.5 %all-reduce.3.cloned.1.call-start = ((), (), s32[]{:S(2)}) async-start(), calls=%async_computation.3 | async-start | bytes 9437184 | tf_op jit(solution)/shard_map/psum | solution.py:71
  323.6 4.6 copy-start.6
  323.6 4.8 copy-start.5
  328.7 7.2 %copy-start.3 = (f32[8192,128]{1,0:T(8,128)S(1)}, f32[8192,128]{1,0:T(8,128)}, u32[]{:S(2)}) copy-start(f32[8192,128]{1,0:T(8,128)} %get-tuple-element.12) | copy-start | bytes 12582916
  335.9 9.9 %copy-start.7 = (f32[4,128,2048]{2,1,0:T(8,128)}, f32[4,128,2048]{2,1,0:T(8,128)S(1)}, u32[]{:S(2)}) copy-start(f32[4,128,2048]{2,1,0:T(8,128)S(1)} %get-tuple-element.30) | copy-start | bytes 12582916
  348.3 1.9 copy-start.2
  392.0 192.9 %all-to-all-start.2 = ((bf16[8,16,128,256]{3,2,1,0:T(8,128)(2,1)}), bf16[8,16,128,256]{3,2,1,0:T(8,128)(2,1)}, u32[]{:S(2)}, u32[]{:S(2)}) async-start(bf16[8,16,128,256]{3,2,1,0:T(8,128)(2,1)} %bitcast.79), calls=%async_computation.2 | async-start | bytes 16777216 | tf_op jit(solution)/shard_map/all_to_all | solution.py:87
  417.6 3.6 copy-start.1
  421.1 117.0 %copy-start.4 = (f32[4096,128]{1,0:T(8,128)S(1)}, f32[4096,128]{1,0:T(8,128)}, u32[]{:S(2)}) copy-start(f32[4096,128]{1,0:T(8,128)} %scatter_custom_fusion.2) | copy-start | bytes 6291460
  427.1 41.1 %collective-permute-start = (f32[256,128]{0,1:T(8,128)S(1)}, f32[256,128]{0,1:T(8,128)S(1)}, u32[]{:S(2)}, u32[]{:S(2)}) collective-permute-start(f32[256,128]{0,1:T(8,128)S(1)} %convolution_add_fusion), channel_id=1, source_target_pairs={{0,4},{4,0},{8,12},{12,8},{16,20},{20,16},{24,28},{28,24},{1,5},{5... | collective-permute-start | bytes 393224 | tf_op jit(solution)/shard_map/ppermute | solution.py:102
  468.2 69.0 %collective-permute-start.1 = (f32[256,128]{0,1:T(8,128)S(1)}, f32[256,128]{0,1:T(8,128)S(1)}, u32[]{:S(2)}, u32[]{:S(2)}) collective-permute-start(f32[256,128]{0,1:T(8,128)S(1)} %add.147), channel_id=1, source_target_pairs={{0,8},{4,12},{8,0},{12,4},{16,24},{20,28},{24,16},{28,20},{1,9},{5... | collective-permute-start | bytes 393224 | tf_op jit(solution)/shard_map/ppermute | solution.py:102
  537.2 46.9 %collective-permute-start.2 = (f32[256,128]{0,1:T(8,128)S(1)}, f32[256,128]{0,1:T(8,128)S(1)}, u32[]{:S(2)}, u32[]{:S(2)}) collective-permute-start(f32[256,128]{0,1:T(8,128)S(1)} %add.148), channel_id=1, source_target_pairs={{0,16},{4,20},{8,24},{12,28},{16,0},{20,4},{24,8},{28,12},{1,17},{... | collective-permute-start | bytes 393224 | tf_op jit(solution)/shard_map/ppermute | solution.py:102
Sparse Core Ops, SparseCore 0:
  228.4 95.0 all-reduce.2
